TPU v7x, 256 devices: a whole 4x4x8 slice. The times are simulated.
256 devices in a mesh: wide: 32 (over z, y_lo, core), narrow: 8 (over x, y_hi).
Axes of the slice: x: 4, y: 4 (y_hi: 2, y_lo: 2; y = y_hi * 2 + y_lo), z: 8, core: 2. Of those that a mesh axis runs over, the one named last changes fastest.
Arguments:
- gradient: bfloat16 [40960, 16384], P(('wide', 'narrow')), may hold values from -81 to 81
- seating: int32 [64], replicated, may hold values from 0 to 63, each once
Outputs:
- rotated: bfloat16 [40960, 16384], P(('wide', 'narrow'))
Inputs may be any that keep to these rules, and one draw needn't show every extreme that they name: `seating`: each of the 64 block numbers is the seat of exactly one block.
All inputs are finite; a program needn't handle non-finite values.
Results may differ from a plain program's by a relative error of at most 0.0075.
Values may be sent and summed in bfloat16 or wider, within the bound.
A program may use at most 64 MiB of HBM per device.

v0:
```python
import jax
import jax.numpy as jnp
from jax import lax
from jax.sharding import PartitionSpec as P

ROUNDS = 8
STEPS = 2


def advance(seat_of, total_slots):
    pair_count = total_slots // 2
    cycle_pos = jnp.where(seat_of % 2 == 0, seat_of // 2 - 1, total_slots - 2 - (seat_of - 1) // 2)
    next_pos = (cycle_pos + 1) % (total_slots - 1)
    new_slot = jnp.where(
        next_pos < pair_count - 1, 2 * (next_pos + 1), 2 * (total_slots - 2 - next_pos) + 1
    )
    return jnp.where(seat_of == 0, 0, new_slot)


def occupants(seat_of, total_slots):
    block_ids = jnp.arange(total_slots, dtype=jnp.int32)
    matches = seat_of[None, :] == block_ids[:, None]
    return jnp.sum(jnp.where(matches, block_ids[None, :], 0), axis=1)


def rotate_columns(matrix, cosine, sine_part):
    width = cosine.shape[0]
    left_cols = matrix[:, :width]
    right_cols = matrix[:, width:]
    return jnp.concatenate(
        [left_cols * cosine - right_cols * sine_part, left_cols * sine_part + right_cols * cosine],
        axis=1,
    )


def roll_second(matrix, offset, which_axis):
    head_part, tail_part = jnp.split(matrix, 2, axis=which_axis)
    return jnp.concatenate(
        [head_part, jnp.roll(tail_part, offset, axis=which_axis)], axis=which_axis
    )


def one_round(round_index, carried):
    gram_mat, rotation = carried
    width = gram_mat.shape[0] // 2
    left_diag = jnp.diagonal(gram_mat[:width, :width])
    right_diag = jnp.diagonal(gram_mat[width:, width:])
    off_diag = jnp.diagonal(gram_mat[:width, width:])
    spread = right_diag - left_diag
    damping = (left_diag + right_diag) / 16.0 + 1e-06
    radius = jnp.sqrt(spread * spread + 4.0 * off_diag * off_diag + damping * damping)
    tangent = 2.0 * off_diag / (spread + radius)
    cosine = 1.0 / jnp.sqrt(1.0 + tangent * tangent)
    sine_part = tangent * cosine
    gram_mat = rotate_columns(gram_mat, cosine, sine_part)
    gram_mat = rotate_columns(gram_mat.T, cosine, sine_part).T
    rotation = rotate_columns(rotation, cosine, sine_part)
    gram_mat = roll_second(roll_second(gram_mat, -1, 0), -1, 1)
    rotation = roll_second(rotation, -1, 1)
    return (gram_mat, rotation)


def rotations(gram_mat):
    initial = (gram_mat, jnp.eye(gram_mat.shape[0], dtype=jnp.float32))
    gram_mat, rotation = lax.fori_loop(0, ROUNDS, one_round, initial)
    return roll_second(rotation, ROUNDS, 1)


def update_pair(paired):
    contract_dims = (((0,), (0,)), ((), ()))
    partial_gram = lax.dot_general(
        paired, paired, contract_dims, preferred_element_type=jnp.float32
    )
    gram_mat = lax.psum(partial_gram, "narrow")
    rotation = rotations(gram_mat).astype(jnp.bfloat16)
    return jnp.dot(paired, rotation, preferred_element_type=jnp.float32).astype(jnp.bfloat16)


def per_device(gradient, seating):
    count_wide = lax.axis_size("wide")
    row_count = gradient.shape[0]
    total_slots = 2 * count_wide
    block_width = gradient.shape[1] // total_slots
    seat_of = seating
    holders = occupants(seat_of, total_slots)
    seated = jnp.take(gradient.reshape(row_count, total_slots, block_width), holders, axis=1)
    seated = seated.reshape(row_count, count_wide, 2, block_width)
    arrived = lax.all_to_all(seated, "wide", split_axis=1, concat_axis=0, tiled=True)
    paired = arrived.reshape(count_wide * row_count, 2 * block_width)
    for section_index in range(STEPS):
        paired = update_pair(paired)
        if section_index + 1 < STEPS:
            following = advance(seat_of, total_slots)
            returned = lax.all_to_all(
                paired.reshape(count_wide * row_count, 1, 2, block_width),
                "wide",
                split_axis=0,
                concat_axis=1,
                tiled=True,
            )
            slotted = returned.reshape(row_count, total_slots, block_width)
            source_slots = jnp.take(seat_of, occupants(following, total_slots))
            regrouped = jnp.take(slotted, source_slots, axis=1).reshape(
                row_count, count_wide, 2, block_width
            )
            arrived = lax.all_to_all(regrouped, "wide", split_axis=1, concat_axis=0, tiled=True)
            paired = arrived.reshape(count_wide * row_count, 2 * block_width)
            seat_of = following
    returned = lax.all_to_all(
        paired.reshape(count_wide * row_count, 1, 2, block_width),
        "wide",
        split_axis=0,
        concat_axis=1,
        tiled=True,
    )
    slotted = returned.reshape(row_count, total_slots, block_width)
    return jnp.take(slotted, seat_of, axis=1).reshape(row_count, total_slots * block_width)


def solution(mesh):
    in_specs = (P(("wide", "narrow"), None), P())
    out_specs = P(("wide", "narrow"), None)
    return jax.shard_map(
        per_device, mesh=mesh, in_specs=in_specs, out_specs=out_specs, check_vma=False
    )
```

profile of v0, /device:TPU:1, one launch (start us, length us, event | category | flops | bytes accessed | tf_op | source)
XLA Modules:
  0.0 1019.4 jit_solution(16833773583891870454)
XLA Ops:
  7.3 5.5 copy.84
  12.9 5.7 gather_fusion.7
  18.6 5.4 broadcast_select_fusion.1
  23.9 10.2 copy.68
  34.1 129.0 %all_to_all.60 = bf16[160,32,2,256]{3,2,0,1:T(2,128)(2,1)S(1)} all-to-all(bf16[160,32,2,256]{3,2,0,1:T(2,128)(2,1)} %copy.68), channel_id=1, replica_groups=mesh['wide'=32,'narrow'=8] {'wide'}, dimensions={1} | all-to-all | bytes 10485760 | tf_op jit(solution)/shard_map/all_to_all | solution.py:88
  164.0 2.3 copy-done.3
  166.3 3.9 fusion.32
  171.4 85.2 %all-reduce.3.cloned.1.call-done = f32[512,512]{1,0:T(8,128)} async-done(((f32[512,512]{1,0:T(8,128)}), f32[512,512]{1,0:T(8,128)}) %all-reduce.3.cloned.1.call-update) | async-done | bytes 1048592 | tf_op jit(solution)/shard_map/psum | solution.py:74
  256.6 103.8 %while.24 = (s32[]{:T(128)}, f32[512,512]{1,0:T(8,128)}, f32[512,512]{0,1:T(8,128)}, s32[]{:T(128)}) while((s32[]{:T(128)}, f32[512,512]{1,0:T(8,128)}, f32[512,512]{0,1:T(8,128)}, s32[]{:T(128)}) %tuple.72), condition=%wide.region_3.5_spmd, body=%wide.region_2.4_spmd.sunk | while | flops 6034946 | bytes 28854352 | solution.py:65
  361.7 7.6 convolution_convert_fusion.1
  369.3 13.6 %copy.69 = bf16[5120,1,2,256]{3,2,1,0:T(2,128)(2,1)} copy(bf16[5120,1,2,256]{0,3,2,1:T(8,128)(2,1)} %bitcast.90) | data formatting | bytes 10485760 | tf_op jit(solution)/shard_map/reshape | solution.py:95
  382.9 12.9 %all-to-all-start.1 = ((bf16[5120,1,2,256]{3,2,1,0:T(2,128)(2,1)}), bf16[5120,1,2,256]{3,2,1,0:T(2,128)(2,1)}, u32[]{:S(2)}, u32[]{:S(2)}) async-start(bf16[5120,1,2,256]{3,2,1,0:T(2,128)(2,1)} %copy.69), calls=%async_computation.1 | async-start | bytes 10485760 | tf_op jit(solution)/shard_map/all_to_all | solution.py:94
  397.1 117.8 %all-to-all-done.1 = bf16[5120,1,2,256]{3,2,1,0:T(2,128)(2,1)} async-done(((bf16[5120,1,2,256]{3,2,1,0:T(2,128)(2,1)}), bf16[5120,1,2,256]{3,2,1,0:T(2,128)(2,1)}, u32[]{:S(2)}, u32[]{:S(2)}) %all-to-all-start.1) | async-done | bytes 5242912 | tf_op jit(solution)/shard_map/all_to_all | solution.py:94
  514.9 3.2 copy.70
  518.0 2.8 copy.71
  520.9 5.7 gather_fusion.8
  526.5 5.4 broadcast_select_fusion
  531.9 10.2 copy.72
  542.1 121.9 %all_to_all.61 = bf16[160,32,2,256]{3,2,0,1:T(2,128)(2,1)S(1)} all-to-all(bf16[160,32,2,256]{3,2,0,1:T(2,128)(2,1)} %copy.72), channel_id=1, replica_groups=mesh['wide'=32,'narrow'=8] {'wide'}, dimensions={1} | all-to-all | bytes 10485760 | tf_op jit(solution)/shard_map/all_to_all | solution.py:106
  664.9 2.3 copy-done.4
  667.2 3.9 fusion.33
  671.1 84.2 %all-reduce.5.cloned.1.call-done = f32[512,512]{1,0:T(8,128)} async-done(((f32[512,512]{1,0:T(8,128)}), f32[512,512]{1,0:T(8,128)}) %all-reduce.5.cloned.1.call-update) | async-done | bytes 1048592 | tf_op jit(solution)/shard_map/psum | solution.py:74
  755.3 86.5 %while.25 = (s32[]{:T(128)}, f32[512,512]{1,0:T(8,128)}, f32[512,512]{0,1:T(8,128)S(1)}, s32[]{:T(128)}) while((s32[]{:T(128)}, f32[512,512]{1,0:T(8,128)}, f32[512,512]{0,1:T(8,128)S(1)}, s32[]{:T(128)}) %tuple.75), condition=%wide.region_7.9_spmd, body=%wide.region_6.8_spmd.sunk | while | flops 6034946 | bytes 28854352 | solution.py:65
  842.0 7.6 convolution_convert_fusion
  849.5 13.6 %copy.73 = bf16[5120,1,2,256]{3,2,1,0:T(2,128)(2,1)} copy(bf16[5120,1,2,256]{0,3,2,1:T(8,128)(2,1)} %bitcast.91) | data formatting | bytes 10485760 | tf_op jit(solution)/shard_map/reshape | solution.py:110
  863.1 12.8 %all-to-all-start.3 = ((bf16[5120,1,2,256]{3,2,1,0:T(2,128)(2,1)}), bf16[5120,1,2,256]{3,2,1,0:T(2,128)(2,1)}, u32[]{:S(2)}, u32[]{:S(2)}) async-start(bf16[5120,1,2,256]{3,2,1,0:T(2,128)(2,1)} %copy.73), calls=%async_computation.3 | async-start | bytes 10485760 | tf_op jit(solution)/shard_map/all_to_all | solution.py:109
  875.9 119.0 %all-to-all-done.3 = bf16[5120,1,2,256]{3,2,1,0:T(2,128)(2,1)} async-done(((bf16[5120,1,2,256]{3,2,1,0:T(2,128)(2,1)}), bf16[5120,1,2,256]{3,2,1,0:T(2,128)(2,1)}, u32[]{:S(2)}, u32[]{:S(2)}) %all-to-all-start.3) | async-done | bytes 5242912 | tf_op jit(solution)/shard_map/all_to_all | solution.py:109
  995.0 3.2 copy.74
  998.2 2.8 copy.75
  1001.0 5.7 gather_fusion.9
  1006.6 3.0 select_bitcast_fusion
  1009.7 2.9 copy.80
  (385 shorter events, 194.4 us)
Async XLA Ops:
  6.5 250.1 %all-reduce.3.cloned.1.call-start = ((), (), s32[]{:S(2)}) async-start(), calls=%async_computation.4 | async-start | bytes 2097152 | tf_op jit(solution)/shard_map/psum | solution.py:74
  164.0 2.4 copy-start.3
  256.6 8.4 copy-start.1
  269.6 8.4 copy-start.1
  282.5 8.4 copy-start.1
  295.5 8.4 copy-start.1
  308.5 8.4 copy-start.1
  321.4 8.4 copy-start.1
  334.4 8.4 copy-start.1
  347.4 8.4 copy-start.1
  382.9 13.2 %copy-start = (s32[64]{0:T(128)S(1)}, s32[64]{0:T(128)}, u32[]{:S(2)}) copy-start(s32[64]{0:T(128)} %param.9) | copy-start | bytes 772
  382.9 132.0 %all-to-all-start.1 = ((bf16[5120,1,2,256]{3,2,1,0:T(2,128)(2,1)}), bf16[5120,1,2,256]{3,2,1,0:T(2,128)(2,1)}, u32[]{:S(2)}, u32[]{:S(2)}) async-start(bf16[5120,1,2,256]{3,2,1,0:T(2,128)(2,1)} %copy.69), calls=%async_computation.1 | async-start | bytes 10485760 | tf_op jit(solution)/shard_map/all_to_all | solution.py:94
  395.8 359.5 %all-reduce.5.cloned.1.call-start = ((), (), s32[]{:S(2)}) async-start(), calls=%async_computation.5 | async-start | bytes 2097152 | tf_op jit(solution)/shard_map/psum | solution.py:74
  664.9 2.4 copy-start.4
  755.3 8.4 copy-start.2
  766.1 8.4 copy-start.2
  776.9 8.4 copy-start.2
  787.7 8.4 copy-start.2
  798.6 8.4 copy-start.2
  809.4 8.4 copy-start.2
  820.2 8.4 copy-start.2
  831.0 8.4 copy-start.2
  863.1 131.8 %all-to-all-start.3 = ((bf16[5120,1,2,256]{3,2,1,0:T(2,128)(2,1)}), bf16[5120,1,2,256]{3,2,1,0:T(2,128)(2,1)}, u32[]{:S(2)}, u32[]{:S(2)}) async-start(bf16[5120,1,2,256]{3,2,1,0:T(2,128)(2,1)} %copy.73), calls=%async_computation.3 | async-start | bytes 10485760 | tf_op jit(solution)/shard_map/all_to_all | solution.py:109
Sparse Core Ops, SparseCore 0:
  170.4 86.1 all-reduce.2
  671.3 83.9 all-reduce.4
where the time goes:
time: 1020 us
  waiting for transfers between devices  406 us (40%)
  blocking collectives  251 us (25%)
  local copies, waits for them, and re-layouts  232 us (23%)
  other arithmetic  65.9 us (6%)
  starting transfers between devices  25.9 us (3%)
  matrix products  22.9 us (2%)
  between operations  13.6 us (1%)
    all_to_all x2, waiting for transfers between devices, per_device(): lax.all_to_all(paired.reshape(count_wide * row_count, 1, 2, block_width),...  237 us
    psum x2, waiting for transfers between devices, update_pair(): gram_mat = lax.psum(partial_gram, 'narrow')  169 us
    all_to_all x1, blocking collectives, per_device(): lax.all_to_all(seated, 'wide', split_axis=1, concat_axis=0, tiled=True)  129 us
    all_to_all x1, blocking collectives, per_device(): lax.all_to_all(regrouped, 'wide', split_axis=1, concat_axis=0, tiled=True)  122 us
    gather x16, local copies, waits for them, and re-layouts, one_round(): off_diag = jnp.diagonal(gram_mat[:width, width:])  37.5 us
    gather x16, local copies, waits for them, and re-layouts, one_round(): right_diag = jnp.diagonal(gram_mat[width:, width:])  37.5 us
    gather x16, local copies, waits for them, and re-layouts, one_round(): left_diag = jnp.diagonal(gram_mat[:width, :width])  37.5 us
    reshape x2, local copies, waits for them, and re-layouts, per_device(): paired.reshape(count_wide * row_count, 1, 2, block_width)  27.2 us
  transfers between devices with their start and end apart: 4, of which 4 were waited for; matrix products, arithmetic and copies ran while one was open for 0% of the time, Pallas kernels for 0%

commit v1 on v0

--- a/solution.py
+++ b/solution.py
@@ -71,7 +71,7 @@
     partial_gram = lax.dot_general(
         paired, paired, contract_dims, preferred_element_type=jnp.float32
     )
-    gram_mat = lax.psum(partial_gram, "narrow")
+    gram_mat = jnp.sum(lax.all_gather(partial_gram, "narrow"), axis=0)
     rotation = rotations(gram_mat).astype(jnp.bfloat16)
     return jnp.dot(paired, rotation, preferred_element_type=jnp.float32).astype(jnp.bfloat16)
 

time: 1020 us -> 1040 us (1.020)
  waiting for transfers between devices: 406 us -> 455 us
  local copies, waits for them, and re-layouts: 232 us -> 213 us
    all_gather x0 -> x2, waiting for transfers between devices: none -> 218 us  [update_pair(): gram_mat = jnp.sum(lax.all_gather(partial_gram, 'narrow'), axis=0)]
    psum x2 -> x0, waiting for transfers between devices: 169 us -> none  [update_pair(): gram_mat = lax.psum(partial_gram, 'narrow')]
    slice x16, local copies, waits for them, and re-layouts: 20 us -> 0.93 us  [one_round(): off_diag = jnp.diagonal(gram_mat[:width, width:])]
    concatenate x32, other arithmetic: 19.7 us -> 3.96 us  [roll_second(): jnp.concatenate([head_part, jnp.roll(tail_part, offset, axis=which_axis)]...]
where the time goes in v1:
time: 1040 us
  waiting for transfers between devices  455 us (44%)
  blocking collectives  252 us (24%)
  local copies, waits for them, and re-layouts  213 us (20%)
  other arithmetic  59.7 us (6%)
  matrix products  23 us (2%)
  starting transfers between devices  17 us (2%)
  between operations  13.9 us (1%)
    all_to_all x2, waiting for transfers between devices, per_device(): lax.all_to_all(paired.reshape(count_wide * row_count, 1, 2, block_width),...  237 us
    all_gather x2, waiting for transfers between devices, update_pair(): gram_mat = jnp.sum(lax.all_gather(partial_gram, 'narrow'), axis=0)  218 us
    all_to_all x1, blocking collectives, per_device(): lax.all_to_all(seated, 'wide', split_axis=1, concat_axis=0, tiled=True)  130 us
    all_to_all x1, blocking collectives, per_device(): lax.all_to_all(regrouped, 'wide', split_axis=1, concat_axis=0, tiled=True)  122 us
    gather x16, local copies, waits for them, and re-layouts, one_round(): left_diag = jnp.diagonal(gram_mat[:width, :width])  37.5 us
    gather x16, local copies, waits for them, and re-layouts, one_round(): off_diag = jnp.diagonal(gram_mat[:width, width:])  37.5 us
    gather x16, local copies, waits for them, and re-layouts, one_round(): right_diag = jnp.diagonal(gram_mat[width:, width:])  37.5 us
    reshape x2, local copies, waits for them, and re-layouts, per_device(): paired.reshape(count_wide * row_count, 1, 2, block_width)  27.2 us
  transfers between devices with their start and end apart: 4, of which 4 were waited for; matrix products, arithmetic and copies ran while one was open for 0% of the time, Pallas kernels for 0%

profile of v1, /device:TPU:1, one launch (start us, length us, event | category | flops | bytes accessed | tf_op | source)
XLA Modules:
  0.0 1036.0 jit_solution(5412475428645500194)
XLA Ops:
  7.3 5.5 copy.84
  12.9 5.7 gather_fusion.7
  18.6 5.4 broadcast_select_fusion.1
  23.9 10.2 copy.68
  34.1 129.6 %all_to_all.60 = bf16[160,32,2,256]{3,2,0,1:T(2,128)(2,1)S(1)} all-to-all(bf16[160,32,2,256]{3,2,0,1:T(2,128)(2,1)} %copy.68), channel_id=1, replica_groups=mesh['wide'=32,'narrow'=8] {'wide'}, dimensions={1} | all-to-all | bytes 10485760 | tf_op jit(solution)/shard_map/all_to_all | solution.py:88
  167.0 3.9 fusion.32
  172.1 109.7 %all-gather.5.cloned.1.call-done = f32[4096,512]{1,0:T(8,128)} async-done(((f32[512,512]{1,0:T(8,128)}), f32[4096,512]{1,0:T(8,128)}) %all-gather.5.cloned.1.call-update) | async-done | bytes 8388624 | tf_op jit(solution)/shard_map/all_gather | solution.py:74
  281.7 4.5 reduce_sum.39
  286.2 87.0 %while.24 = (s32[]{:T(128)}, f32[512,512]{1,0:T(8,128)S(1)}, f32[512,512]{0,1:T(8,128)}, s32[]{:T(128)}) while((s32[]{:T(128)}, f32[512,512]{1,0:T(8,128)S(1)}, f32[512,512]{0,1:T(8,128)}, s32[]{:T(128)}) %tuple.72), condition=%wide.region_3.5_spmd, body=%wide.region_2.4_spmd.sunk | while | flops 6034946 | bytes 24660020 | solution.py:65
  374.6 7.6 convolution_convert_fusion.1
  382.2 13.6 %copy.69 = bf16[5120,1,2,256]{3,2,1,0:T(2,128)(2,1)} copy(bf16[5120,1,2,256]{0,3,2,1:T(8,128)(2,1)} %bitcast.94) | data formatting | bytes 10485760 | tf_op jit(solution)/shard_map/reshape | solution.py:95
  395.8 8.5 all-to-all-start.1
  405.5 117.9 %all-to-all-done.1 = bf16[5120,1,2,256]{3,2,1,0:T(2,128)(2,1)} async-done(((bf16[5120,1,2,256]{3,2,1,0:T(2,128)(2,1)}), bf16[5120,1,2,256]{3,2,1,0:T(2,128)(2,1)}, u32[]{:S(2)}, u32[]{:S(2)}) %all-to-all-start.1) | async-done | bytes 5242912 | tf_op jit(solution)/shard_map/all_to_all | solution.py:94
  523.3 3.2 copy.70
  526.5 2.8 copy.71
  529.3 5.7 gather_fusion.8
  535.0 5.4 broadcast_select_fusion
  540.4 10.2 copy.72
  550.6 122.4 %all_to_all.61 = bf16[160,32,2,256]{3,2,0,1:T(2,128)(2,1)S(1)} all-to-all(bf16[160,32,2,256]{3,2,0,1:T(2,128)(2,1)} %copy.72), channel_id=1, replica_groups=mesh['wide'=32,'narrow'=8] {'wide'}, dimensions={1} | all-to-all | bytes 10485760 | tf_op jit(solution)/shard_map/all_to_all | solution.py:106
  676.2 4.0 fusion.33
  680.2 108.5 %all-gather.7.cloned.1.call-done = f32[4096,512]{1,0:T(8,128)} async-done(((f32[512,512]{1,0:T(8,128)}), f32[4096,512]{1,0:T(8,128)}) %all-gather.7.cloned.1.call-update) | async-done | bytes 8388624 | tf_op jit(solution)/shard_map/all_gather | solution.py:74
  788.7 4.5 reduce_sum.42
  793.2 69.3 %while.25 = (s32[]{:T(128)}, f32[512,512]{1,0:T(8,128)S(1)}, f32[512,512]{0,1:T(8,128)S(1)}, s32[]{:T(128)}) while((s32[]{:T(128)}, f32[512,512]{1,0:T(8,128)S(1)}, f32[512,512]{0,1:T(8,128)S(1)}, s32[]{:T(128)}) %tuple.75), condition=%wide.region_7.9_spmd, body=%wide.region_6.8_spmd.sunk | while | flops 6034946 | bytes 24660020 | solution.py:65
  862.7 7.6 convolution_convert_fusion
  870.3 13.6 %copy.73 = bf16[5120,1,2,256]{3,2,1,0:T(2,128)(2,1)} copy(bf16[5120,1,2,256]{0,3,2,1:T(8,128)(2,1)} %bitcast.95) | data formatting | bytes 10485760 | tf_op jit(solution)/shard_map/reshape | solution.py:110
  883.9 8.3 all-to-all-start.3
  892.2 119.0 %all-to-all-done.3 = bf16[5120,1,2,256]{3,2,1,0:T(2,128)(2,1)} async-done(((bf16[5120,1,2,256]{3,2,1,0:T(2,128)(2,1)}), bf16[5120,1,2,256]{3,2,1,0:T(2,128)(2,1)}, u32[]{:S(2)}, u32[]{:S(2)}) %all-to-all-start.3) | async-done | bytes 5242912 | tf_op jit(solution)/shard_map/all_to_all | solution.py:109
  1011.3 3.2 copy.74
  1014.4 2.8 copy.75
  1017.3 5.7 gather_fusion.9
  1022.9 3.0 select_bitcast_fusion
  1026.0 2.9 copy.80
  (355 shorter events, 164.9 us)
Async XLA Ops:
  6.5 275.2 %all-gather.5.cloned.1.call-start = ((), (), s32[]{:S(2)}) async-start(), calls=%async_computation.4 | async-start | bytes 9437184 | tf_op jit(solution)/shard_map/all_gather | solution.py:74
  164.6 2.4 copy-start.1
  395.8 8.7 copy-start
  395.8 127.5 %all-to-all-start.1 = ((bf16[5120,1,2,256]{3,2,1,0:T(2,128)(2,1)}), bf16[5120,1,2,256]{3,2,1,0:T(2,128)(2,1)}, u32[]{:S(2)}, u32[]{:S(2)}) async-start(bf16[5120,1,2,256]{3,2,1,0:T(2,128)(2,1)} %copy.69), calls=%async_computation.1 | async-start | bytes 10485760 | tf_op jit(solution)/shard_map/all_to_all | solution.py:94
  404.3 384.5 %all-gather.7.cloned.1.call-start = ((), (), s32[]{:S(2)}) async-start(), calls=%async_computation.5 | async-start | bytes 9437184 | tf_op jit(solution)/shard_map/all_gather | solution.py:74
  673.9 2.4 copy-start.2
  883.9 127.4 %all-to-all-start.3 = ((bf16[5120,1,2,256]{3,2,1,0:T(2,128)(2,1)}), bf16[5120,1,2,256]{3,2,1,0:T(2,128)(2,1)}, u32[]{:S(2)}, u32[]{:S(2)}) async-start(bf16[5120,1,2,256]{3,2,1,0:T(2,128)(2,1)} %copy.73), calls=%async_computation.3 | async-start | bytes 10485760 | tf_op jit(solution)/shard_map/all_to_all | solution.py:109
Sparse Core Ops, SparseCore 0:
  171.0 110.6 all-gather.4
  680.3 108.3 all-gather.6
